TPU v7x, 128 devices: a whole 4x4x4 slice. The times are simulated.
128 devices in a mesh: gx: 8 (over x, core), gy: 16 (over z, y).
Axes of the slice: x: 4, y: 4, z: 4, core: 2. Of those that a mesh axis runs over, the one named last changes fastest.
Arguments:
- parent_fields: float32 [5, 4, 384, 6144], P(None, None, 'gx', 'gy'), may hold values from -6 to 6
- parent_velocity: float32 [2, 4, 384, 6144], P(None, None, 'gx', 'gy'), may hold values from -0.3 to 0.3
- parent_mixing: float32 [4, 384, 6144], P(None, 'gx', 'gy'), may hold values from 0.01 to 0.1
- nest_fields: float32 [5, 4, 384, 6144], P(None, None, 'gx', 'gy'), may hold values from -6 to 6
- nest_velocity: float32 [2, 4, 384, 6144], P(None, None, 'gx', 'gy'), may hold values from -0.3 to 0.3
- nest_mixing: float32 [4, 384, 6144], P(None, 'gx', 'gy'), may hold values from 0.01 to 0.1
- nest_anchor: int32 [2], replicated, may hold values from 1 to 3327, as said below
Outputs:
- parent_result: float32 [5, 4, 384, 6144], P(None, None, 'gx', 'gy')
- nest_result: float32 [5, 4, 384, 6144], P(None, None, 'gx', 'gy')
Inputs may be any that keep to these rules, and one draw needn't show every extreme that they name: `nest_anchor`: the row anchor is 1 to 254; the column anchor is 3073 to 3327, so the nest with a rim of one parent cell lies inside the parent grid.
All inputs are finite; a program needn't handle non-finite values.
Results may differ from a plain program's by a relative error of at most 0.00002.
Values sent between devices are 32-bit elements; how exact they have to be, the bound alone decides.
A program may use at most 192 MiB of HBM per device.

v0:
```python
import jax
import jax.numpy as jnp
from jax import lax
from jax.sharding import PartitionSpec as P

SUBSTEPS = 3
third = 1.0 / 3.0
two_thirds = 2.0 / 3.0
nudge_floor = 0.1
relax_width = 4.0


def shift_pairs(count, step):
    return [(i, i + step) for i in range(count) if 0 <= i + step < count]


def neighbours(cells):
    rows = lax.axis_size("gx")
    cols = lax.axis_size("gy")
    western = lax.ppermute(cells[:, :, -1:, :], "gx", shift_pairs(rows, 1))
    eastern = lax.ppermute(cells[:, :, :1, :], "gx", shift_pairs(rows, -1))
    southern = lax.ppermute(cells[:, :, :, -1:], "gy", shift_pairs(cols, 1))
    northern = lax.ppermute(cells[:, :, :, :1], "gy", shift_pairs(cols, -1))
    return (western, eastern, southern, northern)


def update(values, halo, velocity, mixing):
    west_row, east_row, south_col, north_col = halo
    western = jnp.concatenate([west_row, values[:, :, :-1, :]], axis=2)
    eastern = jnp.concatenate([values[:, :, 1:, :], east_row], axis=2)
    southern = jnp.concatenate([south_col, values[:, :, :, :-1]], axis=3)
    northern = jnp.concatenate([values[:, :, :, 1:], north_col], axis=3)
    along_rows = velocity[0]
    along_columns = velocity[1]
    upwind = (
        jnp.maximum(along_rows, 0.0) * (values - western)
        + jnp.minimum(along_rows, 0.0) * (eastern - values)
        + jnp.maximum(along_columns, 0.0) * (values - southern)
        + jnp.minimum(along_columns, 0.0) * (northern - values)
    )
    return values - upwind + mixing * (eastern + western + northern + southern - 4.0 * values)


def refine_rows(block):
    lower = block[:, :, :-2]
    centre = block[:, :, 1:-1]
    upper = block[:, :, 2:]
    stacked = jnp.stack(
        (third * lower + two_thirds * centre, centre, two_thirds * centre + third * upper), axis=3
    )
    extent = centre.shape
    return stacked.reshape(extent[0], extent[1], 3 * extent[2], extent[3])


def refine_columns(block):
    lower = block[:, :, :, :-2]
    centre = block[:, :, :, 1:-1]
    upper = block[:, :, :, 2:]
    stacked = jnp.stack(
        (third * lower + two_thirds * centre, centre, two_thirds * centre + third * upper), axis=4
    )
    extent = centre.shape
    return stacked.reshape(extent[0], extent[1], extent[2], 3 * extent[3])


def block_mean(state):
    extent = state.shape
    grouped = state.reshape(extent[0], extent[1], extent[2] // 3, 3, extent[3] // 3, 3)
    return jnp.sum(grouped, axis=(3, 5)) / 9.0


def relax_weight(row_global, column_global, total_rows, total_columns):
    row_distance = jnp.minimum(row_global, total_rows - 1 - row_global)
    column_distance = jnp.minimum(column_global, total_columns - 1 - column_global)
    distance = jnp.minimum(row_distance[:, None], column_distance[None, :]).astype(jnp.float32)
    return nudge_floor + (1.0 - nudge_floor) * jnp.exp(-distance / relax_width)


def within(positions, limit):
    return (positions >= 0) & (positions < limit)


def column_pairs(count, base, ratio, k, extra):
    pairs = []
    for m in range(count):
        j = ratio * m + k
        p = base + m + extra
        if j < count and p < count:
            pairs.append((p, j))
    return pairs


def per_device(
    parent_fields,
    parent_velocity,
    parent_mixing,
    nest_fields,
    nest_velocity,
    nest_mixing,
    nest_anchor,
):
    row_rank = lax.axis_index("gx")
    column_rank = lax.axis_index("gy")
    row_devices = lax.axis_size("gx")
    column_devices = lax.axis_size("gy")
    parent_rows = parent_fields.shape[2]
    parent_columns = parent_fields.shape[3]
    nest_rows = nest_fields.shape[2]
    nest_columns = nest_fields.shape[3]
    span_rows = nest_rows // 3
    span_columns = nest_columns // 3
    ratio = parent_columns // span_columns
    base = column_devices // 2
    base_column = base * parent_columns
    relay_rows = span_rows + 2
    relay_columns = span_columns + 2
    row_anchor = nest_anchor[0]
    column_anchor = nest_anchor[1]
    offset = column_anchor - 1 - base_column
    parent_next = update(parent_fields, neighbours(parent_fields), parent_velocity, parent_mixing)
    margin = parent_columns - span_columns
    wide = jnp.pad(parent_next, ((0, 0), (0, 0), (0, 0), (margin, margin)))
    relay_cols = None
    for k in range(ratio):
        for extra in (0, 1):
            if extra == 1 and k == 0:
                continue
            start = margin + span_columns * k + offset - extra * parent_columns
            piece = lax.dynamic_slice_in_dim(wide, start, relay_columns, axis=3)
            moved = lax.ppermute(piece, "gy", column_pairs(column_devices, base, ratio, k, extra))
            relay_cols = moved if relay_cols is None else relay_cols + moved
    padded = jnp.pad(relay_cols, ((0, 0), (0, 0), (relay_rows, relay_rows), (0, 0)))
    slots = []
    for target in range(row_devices):
        first = row_anchor - 1 + span_rows * target - parent_rows * row_rank
        first = jnp.clip(first, -relay_rows, parent_rows) + relay_rows
        slots.append(lax.dynamic_slice_in_dim(padded, first, relay_rows, axis=2))
    stacked = jnp.stack(slots, axis=0)
    relay = lax.psum_scatter(stacked, "gx", scatter_dimension=0, tiled=True)[0]
    forcing = refine_columns(refine_rows(relay))
    row_global = row_rank * nest_rows + jnp.arange(nest_rows, dtype=jnp.int32)
    column_global = column_rank * nest_columns + jnp.arange(nest_columns, dtype=jnp.int32)
    weight = relax_weight(
        row_global, column_global, row_devices * nest_rows, column_devices * nest_columns
    )
    state = nest_fields
    for substep in range(SUBSTEPS):
        moved = update(state, neighbours(state), nest_velocity, nest_mixing)
        state = moved + weight * (forcing - moved)
    coarse = block_mean(state)
    gathered = lax.all_gather(coarse, "gx", axis=2, tiled=True)
    total_span = row_devices * span_rows
    gathered = jnp.pad(gathered, ((0, 0), (0, 0), (parent_rows, parent_rows), (0, 0)))
    first = jnp.clip(parent_rows * row_rank - row_anchor, -parent_rows, total_span)
    strip = lax.dynamic_slice_in_dim(gathered, first + parent_rows, parent_rows, axis=2)
    pieces = []
    for extra in (1, 0):
        for k in range(ratio):
            if extra == 1 and k == 0:
                continue
            pairs = [(j, p) for p, j in column_pairs(column_devices, base, ratio, k, extra)]
            pieces.append(lax.ppermute(strip, "gy", pairs))
    joined = jnp.concatenate(pieces, axis=3)
    start = (ratio - 1) * span_columns - 1 - offset
    fed_back = lax.dynamic_slice_in_dim(joined, start, parent_columns, axis=3)
    relative_rows = row_rank * parent_rows + jnp.arange(parent_rows, dtype=jnp.int32) - row_anchor
    relative_columns = (
        column_rank * parent_columns + jnp.arange(parent_columns, dtype=jnp.int32) - column_anchor
    )
    rows_valid = within(relative_rows, total_span)
    columns_valid = within(relative_columns, column_devices * span_columns)
    covered = rows_valid[:, None] & columns_valid[None, :]
    parent_result = jnp.where(covered, fed_back, parent_next)
    return (parent_result, state)


def solution(mesh):
    placed = (
        P(None, None, "gx", "gy"),
        P(None, None, "gx", "gy"),
        P(None, "gx", "gy"),
        P(None, None, "gx", "gy"),
        P(None, None, "gx", "gy"),
        P(None, "gx", "gy"),
        P(),
    )
    return jax.shard_map(
        per_device,
        mesh=mesh,
        in_specs=placed,
        out_specs=(P(None, None, "gx", "gy"), P(None, None, "gx", "gy")),
        check_vma=False,
    )
```

profile of v0, /device:TPU:73, one launch (start us, length us, event | category | flops | bytes accessed | tf_op | source)
XLA Modules:
  0.0 439.8 jit_solution(16195591423806882408)
XLA Ops:
  7.2 2.4 fusion.26
  9.6 3.2 collective-permute-start.6
  12.8 2.1 collective-permute-start.7
  15.6 4.2 collective-permute-start.4
  20.4 1.9 collective-permute-start.5
  22.4 1.8 fusion.25
  24.1 2.1 fusion.27
  26.2 1.1 fusion.22
  28.0 0.9 maximum_bitcast_fusion.1
  41.0 1.4 copy.336
  42.4 1.4 copy.337
  45.4 4.0 multiply_add_fusion.3
  49.4 1.4 pad_dynamic-slice_fusion.3
  50.8 2.1 collective-permute-start.10
  53.0 1.4 collective-permute-start.11
  54.3 1.4 collective-permute-start.12
  55.7 1.9 collective-permute-start.8
  57.6 1.4 collective-permute-start.9
  59.0 0.9 maximum_bitcast_fusion.3
  59.9 1.9 fusion.21
  61.8 11.4 %collective-permute-done.10 = f32[5,4,48,130]{3,2,1,0:T(8,128)S(1)} collective-permute-done((f32[5,4,48,130]{3,2,1,0:T(8,128)S(1)}, f32[5,4,48,130]{3,2,1,0:T(8,128)S(1)}, u32[]{:S(2)}, u32[]{:S(2)}) %collective-permute-start.10) | collective-permute-done | bytes 499232 | tf_op jit(solution)/shard_map/ppermute | solution.py:130
  73.2 8.7 %collective-permute-start.2 = (f32[5,4,48,1]{3,2,1,0:T(8,128)}, f32[5,4,48,1]{3,2,1,0:T(8,128)}, u32[]{:S(2)}, u32[]{:S(2)}) collective-permute-start(f32[5,4,48,1]{3,2,1,0:T(8,128)} %get-tuple-element.30), channel_id=1, source_target_pairs={{0,1},{1,2},{2,3},{3,4},{4,5},{5,6},{6,7},{7,8},{8,9},{9,10},{10,1... | collective-permute-start | bytes 11528 | tf_op jit(solution)/shard_map/ppermute | solution.py:22
  81.9 20.6 %collective-permute-start.3 = (f32[5,4,48,1]{3,2,1,0:T(8,128)}, f32[5,4,48,1]{3,2,1,0:T(8,128)}, u32[]{:S(2)}, u32[]{:S(2)}) collective-permute-start(f32[5,4,48,1]{3,2,1,0:T(8,128)} %get-tuple-element.31), channel_id=1, source_target_pairs={{1,0},{2,1},{3,2},{4,3},{5,4},{6,5},{7,6},{8,7},{9,8},{10,9},{11,1... | collective-permute-start | bytes 11528 | tf_op jit(solution)/shard_map/ppermute | solution.py:23
  102.6 5.0 %collective-permute-start = (f32[5,4,1,384]{3,1,2,0:T(4,128)}, f32[5,4,1,384]{3,1,2,0:T(4,128)}, u32[]{:S(2)}, u32[]{:S(2)}) collective-permute-start(f32[5,4,1,384]{3,1,2,0:T(4,128)} %copy.336), channel_id=1, source_target_pairs={{0,16},{16,32},{32,48},{48,64},{64,80},{80,96},{96,112},{1,17},{17... | collective-permute-start | bytes 92168 | tf_op jit(solution)/shard_map/ppermute | solution.py:20
  107.6 1.9 collective-permute-start.1
  110.9 0.9 bitcast_dynamic-update-slice_fusion.7
  111.8 0.9 bitcast_dynamic-update-slice_fusion.6
  112.6 0.9 bitcast_dynamic-update-slice_fusion.5
  113.5 0.9 bitcast_dynamic-update-slice_fusion.4
  114.4 0.9 bitcast_dynamic-update-slice_fusion.3
  115.3 0.9 bitcast_dynamic-update-slice_fusion.2
  116.2 0.9 bitcast_dynamic-update-slice_fusion.1
  117.1 0.9 bitcast_dynamic-update-slice_fusion
  118.3 2.1 fusion.23
  121.8 1.4 copy.299
  123.1 1.4 copy.301
  124.5 81.9 %all-reduce.6.cloned.1.call-done = f32[8,5,4,18,130]{4,2,3,1,0:T(4,128)} async-done(((f32[8,5,4,18,130]{4,2,3,1,0:T(4,128)}), f32[8,5,4,18,130]{4,2,3,1,0:T(4,128)}) %all-reduce.6.cloned.1.call-update) | async-done | bytes 1497616
  206.4 1.7 dynamic-slice_bitcast_fusion
  209.7 3.6 copy.317
  213.3 3.4 copy.318
  216.8 4.1 multiply_add_fusion.2
  221.4 3.1 collective-permute-start.15
  224.5 2.2 collective-permute-start.16
  226.7 3.6 collective-permute-start.13
  230.4 2.8 collective-permute-start.14
  233.8 2.2 collective-permute-done.14
  236.4 1.8 multiply_add_fusion.1
  238.7 2.9 collective-permute-start.19
  241.5 3.1 collective-permute-start.20
  244.6 5.0 %collective-permute-start.17 = (f32[5,4,1,384]{3,1,2,0:T(4,128)S(1)}, f32[5,4,1,384]{3,1,2,0:T(4,128)S(1)}, u32[]{:S(2)}, u32[]{:S(2)}) collective-permute-start(f32[5,4,1,384]{3,1,2,0:T(4,128)S(1)} %copy.324), channel_id=1, source_target_pairs={{0,16},{16,32},{32,48},{48,64},{64,80},{80,96},{96,112},{1,17},{17... | collective-permute-start | bytes 92168 | tf_op jit(solution)/shard_map/ppermute | solution.py:20
  249.7 1.9 collective-permute-start.18
  252.2 3.0 collective-permute-done.18
  255.3 1.8 multiply_add_fusion
  257.1 60.9 %reshape.74 = f32[5,4,16,3,128,3]{5,4,3,2,1,0:T(8,128)} reshape(f32[5,4,48,384]{3,2,1,0:T(8,128)S(1)} %multiply_add_fusion) | data formatting | bytes 2949120 | tf_op jit(solution)/shard_map/reshape | solution.py:68
  318.0 20.5 %reduce_sum.9 = f32[5,4,16,128]{3,2,1,0:T(8,128)S(1)} reduce(f32[5,4,16,3,128,3]{5,4,3,2,1,0:T(8,128)} %reshape.74, f32[]{:T(128)} %constant.93.clone.1), dimensions={3,5}, to_apply=%region_1.2 | reduce | flops 327680 | bytes 1638404 | tf_op jit(solution)/shard_map/reduce_sum | solution.py:69
  339.9 32.5 %all-gather.2.cloned.1.call-done = f32[5,4,128,128]{3,1,0,2:T(4,128)} async-done(((f32[5,4,16,128]{3,1,0,2:T(4,128)}), f32[5,4,128,128]{3,1,0,2:T(4,128)}) %all-gather.2.cloned.1.call-update) | async-done | bytes 1310736 | tf_op jit(solution)/shard_map/all_gather | solution.py:151
  372.6 1.3 collective-permute-start.21
  373.9 1.3 collective-permute-start.22
  375.9 5.3 %collective-permute-start.23 = (f32[5,4,48,128]{3,2,1,0:T(8,128)S(1)}, f32[5,4,48,128]{3,2,1,0:T(8,128)S(1)}, u32[]{:S(2)}, u32[]{:S(2)}) collective-permute-start(f32[5,4,48,128]{3,2,1,0:T(8,128)S(1)} %copy.330), channel_id=1, source_target_pairs={{0,8},{3,9},{6,10},{9,11},{12,12},{15,13},{16,24},{19,25},{22,26},... | collective-permute-start | bytes 1474568 | tf_op jit(solution)/shard_map/ppermute | solution.py:162
  381.8 1.3 collective-permute-start.24
  383.2 1.3 collective-permute-start.25
  384.5 35.7 %collective-permute-done.21 = f32[5,4,48,128]{3,2,1,0:T(8,128)S(1)} collective-permute-done((f32[5,4,48,128]{3,2,1,0:T(8,128)S(1)}, f32[5,4,48,128]{3,2,1,0:T(8,128)S(1)}, u32[]{:S(2)}, u32[]{:S(2)}) %collective-permute-start.21) | collective-permute-done | bytes 491552 | tf_op jit(solution)/shard_map/ppermute | solution.py:162
  420.4 10.8 %collective-permute-done.25 = f32[5,4,48,128]{3,2,1,0:T(8,128)S(1)} collective-permute-done((f32[5,4,48,128]{3,2,1,0:T(8,128)S(1)}, f32[5,4,48,128]{3,2,1,0:T(8,128)S(1)}, u32[]{:S(2)}, u32[]{:S(2)}) %collective-permute-start.25) | collective-permute-done | bytes 491552 | tf_op jit(solution)/shard_map/ppermute | solution.py:162
  431.3 1.6 dynamic-slice_select_fusion
  (97 shorter events, 13.6 us)
Async XLA Ops:
  7.2 7.7 %copy-start = (f32[5,4,48,384]{3,2,1,0:T(8,128)S(1)}, f32[5,4,48,384]{3,2,1,0:T(8,128)}, u32[]{:S(2)}) copy-start(f32[5,4,48,384]{3,2,1,0:T(8,128)} %param.7) | copy-start | bytes 4423684
  7.2 199.3 %all-reduce.6.cloned.1.call-start = ((), (), s32[]{:S(2)}) async-start(), calls=%async_computation.1 | async-start | bytes 5898240
  9.6 35.7 %collective-permute-start.6 = (f32[5,4,48,1]{3,2,1,0:T(8,128)}, f32[5,4,48,1]{3,2,1,0:T(8,128)}, u32[]{:S(2)}, u32[]{:S(2)}) collective-permute-start(f32[5,4,48,1]{3,2,1,0:T(8,128)} %get-tuple-element.43), channel_id=1, source_target_pairs={{0,1},{1,2},{2,3},{3,4},{4,5},{5,6},{6,7},{7,8},{8,9},{9,10},{10,1... | collective-permute-start | bytes 11528 | tf_op jit(solution)/shard_map/ppermute | solution.py:22
  12.8 32.5 %collective-permute-start.7 = (f32[5,4,48,1]{3,2,1,0:T(8,128)}, f32[5,4,48,1]{3,2,1,0:T(8,128)}, u32[]{:S(2)}, u32[]{:S(2)}) collective-permute-start(f32[5,4,48,1]{3,2,1,0:T(8,128)} %get-tuple-element.44), channel_id=1, source_target_pairs={{1,0},{2,1},{3,2},{4,3},{5,4},{6,5},{7,6},{8,7},{9,8},{10,9},{11,1... | collective-permute-start | bytes 11528 | tf_op jit(solution)/shard_map/ppermute | solution.py:23
  15.6 28.2 %collective-permute-start.4 = (f32[5,4,1,384]{3,1,2,0:T(4,128)}, f32[5,4,1,384]{3,1,2,0:T(4,128)}, u32[]{:S(2)}, u32[]{:S(2)}) collective-permute-start(f32[5,4,1,384]{3,1,2,0:T(4,128)} %copy.338), channel_id=1, source_target_pairs={{0,16},{16,32},{32,48},{48,64},{64,80},{80,96},{96,112},{1,17},{17... | collective-permute-start | bytes 92168 | tf_op jit(solution)/shard_map/ppermute | solution.py:20
  20.4 24.1 %collective-permute-start.5 = (f32[5,4,1,384]{3,1,2,0:T(4,128)}, f32[5,4,1,384]{3,1,2,0:T(4,128)}, u32[]{:S(2)}, u32[]{:S(2)}) collective-permute-start(f32[5,4,1,384]{3,1,2,0:T(4,128)} %copy.339), channel_id=1, source_target_pairs={{16,0},{32,16},{48,32},{64,48},{80,64},{96,80},{112,96},{17,1},{33... | collective-permute-start | bytes 92168 | tf_op jit(solution)/shard_map/ppermute | solution.py:21
  24.1 2.1 copy-start.1
  26.2 1.8 copy-start.9
  26.2 2.7 copy-start.11
  49.4 1.4 copy-start.2
  49.4 9.6 %copy-start.10 = (f32[2,4,48,384]{3,2,1,0:T(8,128)S(1)}, f32[2,4,48,384]{3,2,1,0:T(8,128)}, u32[]{:S(2)}) copy-start(f32[2,4,48,384]{3,2,1,0:T(8,128)} %param.11) | copy-start | bytes 1769476
  50.8 22.4 %collective-permute-start.10 = (f32[5,4,48,130]{3,2,1,0:T(8,128)S(1)}, f32[5,4,48,130]{3,2,1,0:T(8,128)S(1)}, u32[]{:S(2)}, u32[]{:S(2)}) collective-permute-start(f32[5,4,48,130]{3,2,1,0:T(8,128)S(1)} %get-tuple-element.35), channel_id=1, source_target_pairs={{9,1},{10,4},{11,7},{12,10},{13,13},{25,17},{26,20},{27,23},{28,26... | collective-permute-start | bytes 1497608 | tf_op jit(solution)/shard_map/ppermute | solution.py:130
  53.0 29.0 %collective-permute-start.11 = (f32[5,4,48,130]{3,2,1,0:T(8,128)S(1)}, f32[5,4,48,130]{3,2,1,0:T(8,128)S(1)}, u32[]{:S(2)}, u32[]{:S(2)}) collective-permute-start(f32[5,4,48,130]{3,2,1,0:T(8,128)S(1)} %get-tuple-element.36), channel_id=1, source_target_pairs={{8,2},{9,5},{10,8},{11,11},{12,14},{24,18},{25,21},{26,24},{27,27}... | collective-permute-start | bytes 1497608 | tf_op jit(solution)/shard_map/ppermute | solution.py:130
  54.3 48.2 %collective-permute-start.12 = (f32[5,4,48,130]{3,2,1,0:T(8,128)S(1)}, f32[5,4,48,130]{3,2,1,0:T(8,128)S(1)}, u32[]{:S(2)}, u32[]{:S(2)}) collective-permute-start(f32[5,4,48,130]{3,2,1,0:T(8,128)S(1)} %get-tuple-element.37), channel_id=1, source_target_pairs={{9,2},{10,5},{11,8},{12,11},{13,14},{25,18},{26,21},{27,24},{28,27... | collective-permute-start | bytes 1497608 | tf_op jit(solution)/shard_map/ppermute | solution.py:130
  55.7 51.9 %collective-permute-start.8 = (f32[5,4,48,130]{3,2,1,0:T(8,128)S(1)}, f32[5,4,48,130]{3,2,1,0:T(8,128)S(1)}, u32[]{:S(2)}, u32[]{:S(2)}) collective-permute-start(f32[5,4,48,130]{3,2,1,0:T(8,128)S(1)} %get-tuple-element.38), channel_id=1, source_target_pairs={{8,0},{9,3},{10,6},{11,9},{12,12},{13,15},{24,16},{25,19},{26,22},... | collective-permute-start | bytes 1497608 | tf_op jit(solution)/shard_map/ppermute | solution.py:130
  57.6 52.0 %collective-permute-start.9 = (f32[5,4,48,130]{3,2,1,0:T(8,128)S(1)}, f32[5,4,48,130]{3,2,1,0:T(8,128)S(1)}, u32[]{:S(2)}, u32[]{:S(2)}) collective-permute-start(f32[5,4,48,130]{3,2,1,0:T(8,128)S(1)} %get-tuple-element.34), channel_id=1, source_target_pairs={{8,1},{9,4},{10,7},{11,10},{12,13},{24,17},{25,20},{26,23},{27,26}... | collective-permute-start | bytes 1497608 | tf_op jit(solution)/shard_map/ppermute | solution.py:130
  73.2 143.6 %collective-permute-start.2 = (f32[5,4,48,1]{3,2,1,0:T(8,128)}, f32[5,4,48,1]{3,2,1,0:T(8,128)}, u32[]{:S(2)}, u32[]{:S(2)}) collective-permute-start(f32[5,4,48,1]{3,2,1,0:T(8,128)} %get-tuple-element.30), channel_id=1, source_target_pairs={{0,1},{1,2},{2,3},{3,4},{4,5},{5,6},{6,7},{7,8},{8,9},{9,10},{10,1... | collective-permute-start | bytes 11528 | tf_op jit(solution)/shard_map/ppermute | solution.py:22
  81.9 134.8 %collective-permute-start.3 = (f32[5,4,48,1]{3,2,1,0:T(8,128)}, f32[5,4,48,1]{3,2,1,0:T(8,128)}, u32[]{:S(2)}, u32[]{:S(2)}) collective-permute-start(f32[5,4,48,1]{3,2,1,0:T(8,128)} %get-tuple-element.31), channel_id=1, source_target_pairs={{1,0},{2,1},{3,2},{4,3},{5,4},{6,5},{7,6},{8,7},{9,8},{10,9},{11,1... | collective-permute-start | bytes 11528 | tf_op jit(solution)/shard_map/ppermute | solution.py:23
  102.6 19.2 %collective-permute-start = (f32[5,4,1,384]{3,1,2,0:T(4,128)}, f32[5,4,1,384]{3,1,2,0:T(4,128)}, u32[]{:S(2)}, u32[]{:S(2)}) collective-permute-start(f32[5,4,1,384]{3,1,2,0:T(4,128)} %copy.336), channel_id=1, source_target_pairs={{0,16},{16,32},{32,48},{48,64},{64,80},{80,96},{96,112},{1,17},{17... | collective-permute-start | bytes 92168 | tf_op jit(solution)/shard_map/ppermute | solution.py:20
  107.6 15.5 %collective-permute-start.1 = (f32[5,4,1,384]{3,1,2,0:T(4,128)}, f32[5,4,1,384]{3,1,2,0:T(4,128)}, u32[]{:S(2)}, u32[]{:S(2)}) collective-permute-start(f32[5,4,1,384]{3,1,2,0:T(4,128)} %copy.337), channel_id=1, source_target_pairs={{16,0},{32,16},{48,32},{64,48},{80,64},{96,80},{112,96},{17,1},{33... | collective-permute-start | bytes 92168 | tf_op jit(solution)/shard_map/ppermute | solution.py:21
  118.0 254.4 %all-gather.2.cloned.1.call-start = ((), (), s32[]{:S(2)}) async-start(), calls=%async_computation | async-start | bytes 1474560 | tf_op jit(solution)/shard_map/all_gather | solution.py:151
  118.3 2.8 copy-start.12
  221.4 14.6 %collective-permute-start.15 = (f32[5,4,48,1]{3,2,1,0:T(8,128)S(1)}, f32[5,4,48,1]{3,2,1,0:T(8,128)S(1)}, u32[]{:S(2)}, u32[]{:S(2)}) collective-permute-start(f32[5,4,48,1]{3,2,1,0:T(8,128)S(1)} %get-tuple-element.22), channel_id=1, source_target_pairs={{0,1},{1,2},{2,3},{3,4},{4,5},{5,6},{6,7},{7,8},{8,9},{9,10},{10,1... | collective-permute-start | bytes 11528 | tf_op jit(solution)/shard_map/ppermute | solution.py:22
  224.5 11.8 %collective-permute-start.16 = (f32[5,4,48,1]{3,2,1,0:T(8,128)S(1)}, f32[5,4,48,1]{3,2,1,0:T(8,128)S(1)}, u32[]{:S(2)}, u32[]{:S(2)}) collective-permute-start(f32[5,4,48,1]{3,2,1,0:T(8,128)S(1)} %get-tuple-element.23), channel_id=1, source_target_pairs={{1,0},{2,1},{3,2},{4,3},{5,4},{6,5},{7,6},{8,7},{9,8},{10,9},{11,1... | collective-permute-start | bytes 11528 | tf_op jit(solution)/shard_map/ppermute | solution.py:23
  226.7 7.0 %collective-permute-start.13 = (f32[5,4,1,384]{3,1,2,0:T(4,128)S(1)}, f32[5,4,1,384]{3,1,2,0:T(4,128)S(1)}, u32[]{:S(2)}, u32[]{:S(2)}) collective-permute-start(f32[5,4,1,384]{3,1,2,0:T(4,128)S(1)} %copy.319), channel_id=1, source_target_pairs={{0,16},{16,32},{32,48},{48,64},{64,80},{80,96},{96,112},{1,17},{17... | collective-permute-start | bytes 92168 | tf_op jit(solution)/shard_map/ppermute | solution.py:20
  230.3 6.0 %copy-start.5 = (f32[4,48,384]{2,1,0:T(8,128)S(1)}, f32[4,48,384]{2,1,0:T(8,128)}, u32[]{:S(2)}) copy-start(f32[4,48,384]{2,1,0:T(8,128)} %get-tuple-element.60) | copy-start | bytes 884740
  230.4 6.0 %copy-start.6 = (f32[4,48,384]{2,1,0:T(8,128)S(1)}, f32[4,48,384]{2,1,0:T(8,128)}, u32[]{:S(2)}) copy-start(f32[4,48,384]{2,1,0:T(8,128)} %get-tuple-element.61) | copy-start | bytes 884740
  230.4 6.0 %copy-start.7 = (f32[4,48,384]{2,1,0:T(8,128)S(1)}, f32[4,48,384]{2,1,0:T(8,128)}, u32[]{:S(2)}) copy-start(f32[4,48,384]{2,1,0:T(8,128)} %param.12) | copy-start | bytes 884740
  230.4 6.0 %copy-start.8 = (f32[48,384]{1,0:T(8,128)S(1)}, f32[48,384]{1,0:T(8,128)}, u32[]{:S(2)}) copy-start(f32[48,384]{1,0:T(8,128)} %multiply_add_fusion.4) | copy-start | bytes 221188
  230.4 5.6 %collective-permute-start.14 = (f32[5,4,1,384]{3,1,2,0:T(4,128)S(1)}, f32[5,4,1,384]{3,1,2,0:T(4,128)S(1)}, u32[]{:S(2)}, u32[]{:S(2)}) collective-permute-start(f32[5,4,1,384]{3,1,2,0:T(4,128)S(1)} %copy.321), channel_id=1, source_target_pairs={{16,0},{32,16},{48,32},{64,48},{80,64},{96,80},{112,96},{17,1},{33... | collective-permute-start | bytes 92168 | tf_op jit(solution)/shard_map/ppermute | solution.py:21
  238.7 16.6 %collective-permute-start.19 = (f32[5,4,48,1]{3,2,1,0:T(8,128)S(1)}, f32[5,4,48,1]{3,2,1,0:T(8,128)S(1)}, u32[]{:S(2)}, u32[]{:S(2)}) collective-permute-start(f32[5,4,48,1]{3,2,1,0:T(8,128)S(1)} %get-tuple-element.14), channel_id=1, source_target_pairs={{0,1},{1,2},{2,3},{3,4},{4,5},{5,6},{6,7},{7,8},{8,9},{9,10},{10,1... | collective-permute-start | bytes 11528 | tf_op jit(solution)/shard_map/ppermute | solution.py:22
  241.5 13.7 %collective-permute-start.20 = (f32[5,4,48,1]{3,2,1,0:T(8,128)S(1)}, f32[5,4,48,1]{3,2,1,0:T(8,128)S(1)}, u32[]{:S(2)}, u32[]{:S(2)}) collective-permute-start(f32[5,4,48,1]{3,2,1,0:T(8,128)S(1)} %get-tuple-element.15), channel_id=1, source_target_pairs={{1,0},{2,1},{3,2},{4,3},{5,4},{6,5},{7,6},{8,7},{9,8},{10,9},{11,1... | collective-permute-start | bytes 11528 | tf_op jit(solution)/shard_map/ppermute | solution.py:23
  244.6 7.5 %collective-permute-start.17 = (f32[5,4,1,384]{3,1,2,0:T(4,128)S(1)}, f32[5,4,1,384]{3,1,2,0:T(4,128)S(1)}, u32[]{:S(2)}, u32[]{:S(2)}) collective-permute-start(f32[5,4,1,384]{3,1,2,0:T(4,128)S(1)} %copy.324), channel_id=1, source_target_pairs={{0,16},{16,32},{32,48},{48,64},{64,80},{80,96},{96,112},{1,17},{17... | collective-permute-start | bytes 92168 | tf_op jit(solution)/shard_map/ppermute | solution.py:20
  249.7 5.5 %collective-permute-start.18 = (f32[5,4,1,384]{3,1,2,0:T(4,128)S(1)}, f32[5,4,1,384]{3,1,2,0:T(4,128)S(1)}, u32[]{:S(2)}, u32[]{:S(2)}) collective-permute-start(f32[5,4,1,384]{3,1,2,0:T(4,128)S(1)} %copy.326), channel_id=1, source_target_pairs={{16,0},{32,16},{48,32},{64,48},{80,64},{96,80},{112,96},{17,1},{33... | collective-permute-start | bytes 92168 | tf_op jit(solution)/shard_map/ppermute | solution.py:21
  257.1 61.0 %copy-start.4 = (f32[5,4,48,384]{3,2,1,0:T(8,128)}, f32[5,4,48,384]{3,2,1,0:T(8,128)S(1)}, u32[]{:S(2)}) copy-start(f32[5,4,48,384]{3,2,1,0:T(8,128)S(1)} %multiply_add_fusion) | copy-start | bytes 4423684
  372.6 47.6 %collective-permute-start.21 = (f32[5,4,48,128]{3,2,1,0:T(8,128)S(1)}, f32[5,4,48,128]{3,2,1,0:T(8,128)S(1)}, u32[]{:S(2)}, u32[]{:S(2)}) collective-permute-start(f32[5,4,48,128]{3,2,1,0:T(8,128)S(1)} %copy.330), channel_id=1, source_target_pairs={{1,9},{4,10},{7,11},{10,12},{13,13},{17,25},{20,26},{23,27},{26,28... | collective-permute-start | bytes 1474568 | tf_op jit(solution)/shard_map/ppermute | solution.py:162
  373.9 46.4 %collective-permute-start.22 = (f32[5,4,48,128]{3,2,1,0:T(8,128)S(1)}, f32[5,4,48,128]{3,2,1,0:T(8,128)S(1)}, u32[]{:S(2)}, u32[]{:S(2)}) collective-permute-start(f32[5,4,48,128]{3,2,1,0:T(8,128)S(1)} %copy.330), channel_id=1, source_target_pairs={{2,9},{5,10},{8,11},{11,12},{14,13},{18,25},{21,26},{24,27},{27,28... | collective-permute-start | bytes 1474568 | tf_op jit(solution)/shard_map/ppermute | solution.py:162
  375.9 44.5 %collective-permute-start.23 = (f32[5,4,48,128]{3,2,1,0:T(8,128)S(1)}, f32[5,4,48,128]{3,2,1,0:T(8,128)S(1)}, u32[]{:S(2)}, u32[]{:S(2)}) collective-permute-start(f32[5,4,48,128]{3,2,1,0:T(8,128)S(1)} %copy.330), channel_id=1, source_target_pairs={{0,8},{3,9},{6,10},{9,11},{12,12},{15,13},{16,24},{19,25},{22,26},... | collective-permute-start | bytes 1474568 | tf_op jit(solution)/shard_map/ppermute | solution.py:162
  381.8 38.6 %collective-permute-start.24 = (f32[5,4,48,128]{3,2,1,0:T(8,128)S(1)}, f32[5,4,48,128]{3,2,1,0:T(8,128)S(1)}, u32[]{:S(2)}, u32[]{:S(2)}) collective-permute-start(f32[5,4,48,128]{3,2,1,0:T(8,128)S(1)} %copy.330), channel_id=1, source_target_pairs={{1,8},{4,9},{7,10},{10,11},{13,12},{17,24},{20,25},{23,26},{26,27}... | collective-permute-start | bytes 1474568 | tf_op jit(solution)/shard_map/ppermute | solution.py:162
  383.2 48.1 %collective-permute-start.25 = (f32[5,4,48,128]{3,2,1,0:T(8,128)S(1)}, f32[5,4,48,128]{3,2,1,0:T(8,128)S(1)}, u32[]{:S(2)}, u32[]{:S(2)}) collective-permute-start(f32[5,4,48,128]{3,2,1,0:T(8,128)S(1)} %copy.330), channel_id=1, source_target_pairs={{2,8},{5,9},{8,10},{11,11},{14,12},{18,24},{21,25},{24,26},{27,27}... | collective-permute-start | bytes 1474568 | tf_op jit(solution)/shard_map/ppermute | solution.py:162
  420.3 11.0 %copy-start.3 = (f32[5,4,48,384]{3,2,1,0:T(8,128)S(1)}, f32[5,4,48,384]{3,2,1,0:T(8,128)}, u32[]{:S(2)}) copy-start(f32[5,4,48,384]{3,2,1,0:T(8,128)} %copy-done.2) | copy-start | bytes 4423684
Sparse Core Ops, SparseCore 0:
  118.2 88.2 all-reduce.5
  339.4 32.9 all-gather.1
where the time goes:
time: 441 us; the launch traced here: 440 us
  waiting for transfers between devices  178 us (40%)
  local copies, waits for them, and re-layouts  104 us (24%)
  starting transfers between devices  91.2 us (21%)
  other arithmetic  39.5 us (9%)
  between operations  27 us (6%)
    unnamed x3, waiting for transfers between devices  81.9 us
    reshape x1, local copies, waits for them, and re-layouts, block_mean(): state.reshape(extent[0], extent[1], extent[2] // 3, 3, extent[3] // 3, 3)  60.9 us
    ppermute x5, waiting for transfers between devices, per_device(): pieces.append(lax.ppermute(strip, 'gy', pairs))  46.6 us
    all_gather x1, waiting for transfers between devices, per_device(): gathered = lax.all_gather(coarse, 'gx', axis=2, tiled=True)  32.5 us
    ppermute x4, starting transfers between devices, neighbours(): northern = lax.ppermute(cells[:, :, :, :1], 'gy', shift_pairs(cols, -1))  28 us
    reduce_sum x1, other arithmetic, block_mean(): return jnp.sum(grouped, axis=(3, 5)) / 9.0  20.5 us
    ppermute x4, starting transfers between devices, neighbours(): southern = lax.ppermute(cells[:, :, :, -1:], 'gy', shift_pairs(cols, 1))  17.9 us
    ppermute x4, starting transfers between devices, neighbours(): western = lax.ppermute(cells[:, :, -1:, :], 'gx', shift_pairs(rows, 1))  17.9 us
  transfers between devices with their start and end apart: 28, of which 8 were waited for; matrix products, arithmetic and copies ran while one was open for 10% of the time, Pallas kernels for 0%

commit v1 on v0

--- a/solution.py
+++ b/solution.py
@@ -148,7 +148,8 @@
         moved = update(state, neighbours(state), nest_velocity, nest_mixing)
         state = moved + weight * (forcing - moved)
     coarse = block_mean(state)
-    gathered = lax.all_gather(coarse, "gx", axis=2, tiled=True)
+    copies = jnp.concatenate([coarse] * lax.axis_size("gx"), axis=2)
+    gathered = lax.all_to_all(copies, "gx", 2, 2, tiled=True)
     total_span = row_devices * span_rows
     gathered = jnp.pad(gathered, ((0, 0), (0, 0), (parent_rows, parent_rows), (0, 0)))
     first = jnp.clip(parent_rows * row_rank - row_anchor, -parent_rows, total_span)

time: 441 us -> 439 us (level)
  waiting for transfers between devices: 178 us -> 162 us
  starting transfers between devices: 91.2 us -> 103 us
    all_gather x1 -> x0, waiting for transfers between devices: 32.5 us -> none  [per_device(): gathered = lax.all_gather(coarse, 'gx', axis=2, tiled=True)]
    all_to_all x0 -> x1, waiting for transfers between devices: none -> 17.3 us  [per_device(): gathered = lax.all_to_all(copies, 'gx', 2, 2, tiled=True)]
    all_to_all x0 -> x1, starting transfers between devices: none -> 11 us  [per_device(): gathered = lax.all_to_all(copies, 'gx', 2, 2, tiled=True)]
    unnamed x3 -> x2, waiting for transfers between devices: 81.9 us -> 82 us
where the time goes in v1:
time: 439 us; the launch traced here: 438 us
  waiting for transfers between devices  162 us (37%)
  local copies, waits for them, and re-layouts  106 us (24%)
  starting transfers between devices  103 us (23%)
  other arithmetic  39.6 us (9%)
  between operations  26.9 us (6%)
    unnamed x2, waiting for transfers between devices  82 us
    reshape x1, local copies, waits for them, and re-layouts, block_mean(): state.reshape(extent[0], extent[1], extent[2] // 3, 3, extent[3] // 3, 3)  60.9 us
    ppermute x5, waiting for transfers between devices, per_device(): pieces.append(lax.ppermute(strip, 'gy', pairs))  46.1 us
    ppermute x4, starting transfers between devices, neighbours(): northern = lax.ppermute(cells[:, :, :, :1], 'gy', shift_pairs(cols, -1))  28 us
    reduce_sum x1, other arithmetic, block_mean(): return jnp.sum(grouped, axis=(3, 5)) / 9.0  20.5 us
    ppermute x4, starting transfers between devices, neighbours(): southern = lax.ppermute(cells[:, :, :, -1:], 'gy', shift_pairs(cols, 1))  17.9 us
    ppermute x4, starting transfers between devices, neighbours(): western = lax.ppermute(cells[:, :, -1:, :], 'gx', shift_pairs(rows, 1))  17.9 us
    all_to_all x1, waiting for transfers between devices, per_device(): gathered = lax.all_to_all(copies, 'gx', 2, 2, tiled=True)  17.3 us
  transfers between devices with their start and end apart: 28, of which 8 were waited for; matrix products, arithmetic and copies ran while one was open for 10% of the time, Pallas kernels for 0%

profile of v1, /device:TPU:73, one launch (start us, length us, event | category | flops | bytes accessed | tf_op | source)
XLA Modules:
  0.0 437.8 jit_solution(13969954149878112049)
XLA Ops:
  7.2 2.4 fusion.26
  9.6 3.2 collective-permute-start.6
  12.8 2.1 collective-permute-start.7
  15.6 4.2 collective-permute-start.4
  20.4 1.9 collective-permute-start.5
  22.3 1.8 fusion.25
  24.1 2.1 fusion.27
  26.2 1.1 fusion.22
  28.0 0.9 maximum_bitcast_fusion.1
  40.9 1.4 copy.445
  42.2 1.4 copy.446
  45.2 4.0 multiply_add_fusion.3
  49.3 1.4 pad_dynamic-slice_fusion.3
  50.7 2.1 collective-permute-start.10
  52.8 1.4 collective-permute-start.11
  54.2 1.4 collective-permute-start.12
  55.5 1.9 collective-permute-start.8
  57.5 1.4 collective-permute-start.9
  58.8 0.9 maximum_bitcast_fusion.3
  59.7 1.9 fusion.21
  61.6 11.4 %collective-permute-done.10 = f32[5,4,48,130]{3,2,1,0:T(8,128)S(1)} collective-permute-done((f32[5,4,48,130]{3,2,1,0:T(8,128)S(1)}, f32[5,4,48,130]{3,2,1,0:T(8,128)S(1)}, u32[]{:S(2)}, u32[]{:S(2)}) %collective-permute-start.10) | collective-permute-done | bytes 499232 | tf_op jit(solution)/shard_map/ppermute | solution.py:130
  73.0 8.8 %collective-permute-start.2 = (f32[5,4,48,1]{3,2,1,0:T(8,128)}, f32[5,4,48,1]{3,2,1,0:T(8,128)}, u32[]{:S(2)}, u32[]{:S(2)}) collective-permute-start(f32[5,4,48,1]{3,2,1,0:T(8,128)} %get-tuple-element.32), channel_id=1, source_target_pairs={{0,1},{1,2},{2,3},{3,4},{4,5},{5,6},{6,7},{7,8},{8,9},{9,10},{10,1... | collective-permute-start | bytes 11528 | tf_op jit(solution)/shard_map/ppermute | solution.py:22
  81.8 20.6 %collective-permute-start.3 = (f32[5,4,48,1]{3,2,1,0:T(8,128)}, f32[5,4,48,1]{3,2,1,0:T(8,128)}, u32[]{:S(2)}, u32[]{:S(2)}) collective-permute-start(f32[5,4,48,1]{3,2,1,0:T(8,128)} %get-tuple-element.33), channel_id=1, source_target_pairs={{1,0},{2,1},{3,2},{4,3},{5,4},{6,5},{7,6},{8,7},{9,8},{10,9},{11,1... | collective-permute-start | bytes 11528 | tf_op jit(solution)/shard_map/ppermute | solution.py:23
  102.4 5.1 %collective-permute-start = (f32[5,4,1,384]{3,1,2,0:T(4,128)}, f32[5,4,1,384]{3,1,2,0:T(4,128)}, u32[]{:S(2)}, u32[]{:S(2)}) collective-permute-start(f32[5,4,1,384]{3,1,2,0:T(4,128)} %copy.445), channel_id=1, source_target_pairs={{0,16},{16,32},{32,48},{48,64},{64,80},{80,96},{96,112},{1,17},{17... | collective-permute-start | bytes 92168 | tf_op jit(solution)/shard_map/ppermute | solution.py:20
  107.5 2.1 collective-permute-start.1
  112.7 0.9 bitcast_dynamic-update-slice_fusion.5
  114.4 0.9 bitcast_dynamic-update-slice_fusion.3
  115.3 0.9 bitcast_dynamic-update-slice_fusion.2
  116.2 0.9 bitcast_dynamic-update-slice_fusion.1
  117.1 0.9 bitcast_dynamic-update-slice_fusion
  118.1 2.1 fusion.23
  121.5 1.4 copy.408
  122.9 1.4 copy.410
  124.3 82.0 %all-reduce.6.cloned.1.call-done = f32[8,5,4,18,130]{4,2,3,1,0:T(4,128)} async-done(((f32[8,5,4,18,130]{4,2,3,1,0:T(4,128)}), f32[8,5,4,18,130]{4,2,3,1,0:T(4,128)}) %all-reduce.6.cloned.1.call-update) | async-done | bytes 1497616
  206.3 1.6 dynamic-slice_bitcast_fusion
  209.5 3.6 copy.426
  213.1 3.4 copy.427
  216.5 4.1 multiply_add_fusion.2
  221.2 3.1 collective-permute-start.15
  224.3 2.2 collective-permute-start.16
  226.5 3.6 collective-permute-start.13
  230.1 2.8 collective-permute-start.14
  233.5 2.2 collective-permute-done.14
  236.1 1.8 multiply_add_fusion.1
  238.4 2.9 collective-permute-start.19
  241.3 3.1 collective-permute-start.20
  244.4 5.0 %collective-permute-start.17 = (f32[5,4,1,384]{3,1,2,0:T(4,128)S(1)}, f32[5,4,1,384]{3,1,2,0:T(4,128)S(1)}, u32[]{:S(2)}, u32[]{:S(2)}) collective-permute-start(f32[5,4,1,384]{3,1,2,0:T(4,128)S(1)} %copy.433), channel_id=1, source_target_pairs={{0,16},{16,32},{32,48},{48,64},{64,80},{80,96},{96,112},{1,17},{17... | collective-permute-start | bytes 92168 | tf_op jit(solution)/shard_map/ppermute | solution.py:20
  249.5 2.1 collective-permute-start.18
  252.2 2.8 collective-permute-done.18
  255.0 1.8 multiply_add_fusion
  256.8 1.1 copy-done.4
  257.9 60.9 %reshape.74 = f32[5,4,16,3,128,3]{5,4,3,2,1,0:T(8,128)} reshape(f32[5,4,48,384]{3,2,1,0:T(8,128)S(1)} %multiply_add_fusion) | data formatting | bytes 2949120 | tf_op jit(solution)/shard_map/reshape | solution.py:68
  318.9 20.5 %reduce_sum.9 = f32[5,4,16,128]{3,2,1,0:T(8,128)S(1)} reduce(f32[5,4,16,3,128,3]{5,4,3,2,1,0:T(8,128)} %reshape.74, f32[]{:T(128)} %constant.93.clone.1), dimensions={3,5}, to_apply=%region_1.2 | reduce | flops 327680 | bytes 1638404 | tf_op jit(solution)/shard_map/reduce_sum | solution.py:69
  339.5 1.9 copy.438
  341.5 11.0 %all-to-all-start = ((f32[5,4,128,128]{3,1,0,2:T(4,128)}), f32[5,4,128,128]{3,1,0,2:T(4,128)S(1)}, u32[]{:S(2)}, u32[]{:S(2)}) async-start(f32[5,4,128,128]{3,1,0,2:T(4,128)} %copy.438), calls=%async_computation | async-start | bytes 2621440 | tf_op jit(solution)/shard_map/all_to_all | solution.py:152
  353.1 17.3 %all-to-all-done = f32[5,4,128,128]{3,1,0,2:T(4,128)S(1)} async-done(((f32[5,4,128,128]{3,1,0,2:T(4,128)}), f32[5,4,128,128]{3,1,0,2:T(4,128)S(1)}, u32[]{:S(2)}, u32[]{:S(2)}) %all-to-all-start) | async-done | bytes 1310752 | tf_op jit(solution)/shard_map/all_to_all | solution.py:152
  370.6 1.3 collective-permute-start.21
  371.9 1.3 collective-permute-start.22
  373.9 5.8 %collective-permute-start.23 = (f32[5,4,48,128]{3,2,1,0:T(8,128)S(1)}, f32[5,4,48,128]{3,2,1,0:T(8,128)S(1)}, u32[]{:S(2)}, u32[]{:S(2)}) collective-permute-start(f32[5,4,48,128]{3,2,1,0:T(8,128)S(1)} %copy.439), channel_id=1, source_target_pairs={{0,8},{3,9},{6,10},{9,11},{12,12},{15,13},{16,24},{19,25},{22,26},... | collective-permute-start | bytes 1474568 | tf_op jit(solution)/shard_map/ppermute | solution.py:163
  380.3 1.3 collective-permute-start.24
  381.7 1.3 collective-permute-start.25
  383.0 34.5 %collective-permute-done.21 = f32[5,4,48,128]{3,2,1,0:T(8,128)S(1)} collective-permute-done((f32[5,4,48,128]{3,2,1,0:T(8,128)S(1)}, f32[5,4,48,128]{3,2,1,0:T(8,128)S(1)}, u32[]{:S(2)}, u32[]{:S(2)}) %collective-permute-start.21) | collective-permute-done | bytes 491552 | tf_op jit(solution)/shard_map/ppermute | solution.py:163
  417.7 11.6 %collective-permute-done.25 = f32[5,4,48,128]{3,2,1,0:T(8,128)S(1)} collective-permute-done((f32[5,4,48,128]{3,2,1,0:T(8,128)S(1)}, f32[5,4,48,128]{3,2,1,0:T(8,128)S(1)}, u32[]{:S(2)}, u32[]{:S(2)}) %collective-permute-start.25) | collective-permute-done | bytes 491552 | tf_op jit(solution)/shard_map/ppermute | solution.py:163
  429.3 1.6 dynamic-slice_select_fusion
  (103 shorter events, 15.4 us)
Async XLA Ops:
  7.2 7.7 %copy-start = (f32[5,4,48,384]{3,2,1,0:T(8,128)S(1)}, f32[5,4,48,384]{3,2,1,0:T(8,128)}, u32[]{:S(2)}) copy-start(f32[5,4,48,384]{3,2,1,0:T(8,128)} %param.7) | copy-start | bytes 4423684
  7.2 199.1 %all-reduce.6.cloned.1.call-start = ((), (), s32[]{:S(2)}) async-start(), calls=%async_computation.1 | async-start | bytes 5898240
  9.6 35.6 %collective-permute-start.6 = (f32[5,4,48,1]{3,2,1,0:T(8,128)}, f32[5,4,48,1]{3,2,1,0:T(8,128)}, u32[]{:S(2)}, u32[]{:S(2)}) collective-permute-start(f32[5,4,48,1]{3,2,1,0:T(8,128)} %get-tuple-element.45), channel_id=1, source_target_pairs={{0,1},{1,2},{2,3},{3,4},{4,5},{5,6},{6,7},{7,8},{8,9},{9,10},{10,1... | collective-permute-start | bytes 11528 | tf_op jit(solution)/shard_map/ppermute | solution.py:22
  12.8 32.4 %collective-permute-start.7 = (f32[5,4,48,1]{3,2,1,0:T(8,128)}, f32[5,4,48,1]{3,2,1,0:T(8,128)}, u32[]{:S(2)}, u32[]{:S(2)}) collective-permute-start(f32[5,4,48,1]{3,2,1,0:T(8,128)} %get-tuple-element.46), channel_id=1, source_target_pairs={{1,0},{2,1},{3,2},{4,3},{5,4},{6,5},{7,6},{8,7},{9,8},{10,9},{11,1... | collective-permute-start | bytes 11528 | tf_op jit(solution)/shard_map/ppermute | solution.py:23
  15.6 28.1 %collective-permute-start.4 = (f32[5,4,1,384]{3,1,2,0:T(4,128)}, f32[5,4,1,384]{3,1,2,0:T(4,128)}, u32[]{:S(2)}, u32[]{:S(2)}) collective-permute-start(f32[5,4,1,384]{3,1,2,0:T(4,128)} %copy.447), channel_id=1, source_target_pairs={{0,16},{16,32},{32,48},{48,64},{64,80},{80,96},{96,112},{1,17},{17... | collective-permute-start | bytes 92168 | tf_op jit(solution)/shard_map/ppermute | solution.py:20
  20.4 24.0 %collective-permute-start.5 = (f32[5,4,1,384]{3,1,2,0:T(4,128)}, f32[5,4,1,384]{3,1,2,0:T(4,128)}, u32[]{:S(2)}, u32[]{:S(2)}) collective-permute-start(f32[5,4,1,384]{3,1,2,0:T(4,128)} %copy.448), channel_id=1, source_target_pairs={{16,0},{32,16},{48,32},{64,48},{80,64},{96,80},{112,96},{17,1},{33... | collective-permute-start | bytes 92168 | tf_op jit(solution)/shard_map/ppermute | solution.py:21
  24.1 2.1 copy-start.1
  26.2 1.8 copy-start.9
  26.2 2.7 copy-start.11
  49.3 1.4 copy-start.2
  49.3 9.6 %copy-start.10 = (f32[2,4,48,384]{3,2,1,0:T(8,128)S(1)}, f32[2,4,48,384]{3,2,1,0:T(8,128)}, u32[]{:S(2)}) copy-start(f32[2,4,48,384]{3,2,1,0:T(8,128)} %param.11) | copy-start | bytes 1769476
  50.7 22.3 %collective-permute-start.10 = (f32[5,4,48,130]{3,2,1,0:T(8,128)S(1)}, f32[5,4,48,130]{3,2,1,0:T(8,128)S(1)}, u32[]{:S(2)}, u32[]{:S(2)}) collective-permute-start(f32[5,4,48,130]{3,2,1,0:T(8,128)S(1)} %get-tuple-element.37), channel_id=1, source_target_pairs={{9,1},{10,4},{11,7},{12,10},{13,13},{25,17},{26,20},{27,23},{28,26... | collective-permute-start | bytes 1497608 | tf_op jit(solution)/shard_map/ppermute | solution.py:130
  52.8 29.0 %collective-permute-start.11 = (f32[5,4,48,130]{3,2,1,0:T(8,128)S(1)}, f32[5,4,48,130]{3,2,1,0:T(8,128)S(1)}, u32[]{:S(2)}, u32[]{:S(2)}) collective-permute-start(f32[5,4,48,130]{3,2,1,0:T(8,128)S(1)} %get-tuple-element.38), channel_id=1, source_target_pairs={{8,2},{9,5},{10,8},{11,11},{12,14},{24,18},{25,21},{26,24},{27,27}... | collective-permute-start | bytes 1497608 | tf_op jit(solution)/shard_map/ppermute | solution.py:130
  54.2 48.2 %collective-permute-start.12 = (f32[5,4,48,130]{3,2,1,0:T(8,128)S(1)}, f32[5,4,48,130]{3,2,1,0:T(8,128)S(1)}, u32[]{:S(2)}, u32[]{:S(2)}) collective-permute-start(f32[5,4,48,130]{3,2,1,0:T(8,128)S(1)} %get-tuple-element.39), channel_id=1, source_target_pairs={{9,2},{10,5},{11,8},{12,11},{13,14},{25,18},{26,21},{27,24},{28,27... | collective-permute-start | bytes 1497608 | tf_op jit(solution)/shard_map/ppermute | solution.py:130
  55.5 52.0 %collective-permute-start.8 = (f32[5,4,48,130]{3,2,1,0:T(8,128)S(1)}, f32[5,4,48,130]{3,2,1,0:T(8,128)S(1)}, u32[]{:S(2)}, u32[]{:S(2)}) collective-permute-start(f32[5,4,48,130]{3,2,1,0:T(8,128)S(1)} %get-tuple-element.40), channel_id=1, source_target_pairs={{8,0},{9,3},{10,6},{11,9},{12,12},{13,15},{24,16},{25,19},{26,22},... | collective-permute-start | bytes 1497608 | tf_op jit(solution)/shard_map/ppermute | solution.py:130
  57.5 52.2 %collective-permute-start.9 = (f32[5,4,48,130]{3,2,1,0:T(8,128)S(1)}, f32[5,4,48,130]{3,2,1,0:T(8,128)S(1)}, u32[]{:S(2)}, u32[]{:S(2)}) collective-permute-start(f32[5,4,48,130]{3,2,1,0:T(8,128)S(1)} %get-tuple-element.36), channel_id=1, source_target_pairs={{8,1},{9,4},{10,7},{11,10},{12,13},{24,17},{25,20},{26,23},{27,26}... | collective-permute-start | bytes 1497608 | tf_op jit(solution)/shard_map/ppermute | solution.py:130
  73.0 143.5 %collective-permute-start.2 = (f32[5,4,48,1]{3,2,1,0:T(8,128)}, f32[5,4,48,1]{3,2,1,0:T(8,128)}, u32[]{:S(2)}, u32[]{:S(2)}) collective-permute-start(f32[5,4,48,1]{3,2,1,0:T(8,128)} %get-tuple-element.32), channel_id=1, source_target_pairs={{0,1},{1,2},{2,3},{3,4},{4,5},{5,6},{6,7},{7,8},{8,9},{9,10},{10,1... | collective-permute-start | bytes 11528 | tf_op jit(solution)/shard_map/ppermute | solution.py:22
  81.8 134.7 %collective-permute-start.3 = (f32[5,4,48,1]{3,2,1,0:T(8,128)}, f32[5,4,48,1]{3,2,1,0:T(8,128)}, u32[]{:S(2)}, u32[]{:S(2)}) collective-permute-start(f32[5,4,48,1]{3,2,1,0:T(8,128)} %get-tuple-element.33), channel_id=1, source_target_pairs={{1,0},{2,1},{3,2},{4,3},{5,4},{6,5},{7,6},{8,7},{9,8},{10,9},{11,1... | collective-permute-start | bytes 11528 | tf_op jit(solution)/shard_map/ppermute | solution.py:23
  102.4 19.1 %collective-permute-start = (f32[5,4,1,384]{3,1,2,0:T(4,128)}, f32[5,4,1,384]{3,1,2,0:T(4,128)}, u32[]{:S(2)}, u32[]{:S(2)}) collective-permute-start(f32[5,4,1,384]{3,1,2,0:T(4,128)} %copy.445), channel_id=1, source_target_pairs={{0,16},{16,32},{32,48},{48,64},{64,80},{80,96},{96,112},{1,17},{17... | collective-permute-start | bytes 92168 | tf_op jit(solution)/shard_map/ppermute | solution.py:20
  107.5 15.4 %collective-permute-start.1 = (f32[5,4,1,384]{3,1,2,0:T(4,128)}, f32[5,4,1,384]{3,1,2,0:T(4,128)}, u32[]{:S(2)}, u32[]{:S(2)}) collective-permute-start(f32[5,4,1,384]{3,1,2,0:T(4,128)} %copy.446), channel_id=1, source_target_pairs={{16,0},{32,16},{48,32},{64,48},{80,64},{96,80},{112,96},{17,1},{33... | collective-permute-start | bytes 92168 | tf_op jit(solution)/shard_map/ppermute | solution.py:21
  118.1 2.8 copy-start.12
  221.2 14.6 %collective-permute-start.15 = (f32[5,4,48,1]{3,2,1,0:T(8,128)S(1)}, f32[5,4,48,1]{3,2,1,0:T(8,128)S(1)}, u32[]{:S(2)}, u32[]{:S(2)}) collective-permute-start(f32[5,4,48,1]{3,2,1,0:T(8,128)S(1)} %get-tuple-element.24), channel_id=1, source_target_pairs={{0,1},{1,2},{2,3},{3,4},{4,5},{5,6},{6,7},{7,8},{8,9},{9,10},{10,1... | collective-permute-start | bytes 11528 | tf_op jit(solution)/shard_map/ppermute | solution.py:22
  224.3 11.8 %collective-permute-start.16 = (f32[5,4,48,1]{3,2,1,0:T(8,128)S(1)}, f32[5,4,48,1]{3,2,1,0:T(8,128)S(1)}, u32[]{:S(2)}, u32[]{:S(2)}) collective-permute-start(f32[5,4,48,1]{3,2,1,0:T(8,128)S(1)} %get-tuple-element.25), channel_id=1, source_target_pairs={{1,0},{2,1},{3,2},{4,3},{5,4},{6,5},{7,6},{8,7},{9,8},{10,9},{11,1... | collective-permute-start | bytes 11528 | tf_op jit(solution)/shard_map/ppermute | solution.py:23
  226.5 7.0 %collective-permute-start.13 = (f32[5,4,1,384]{3,1,2,0:T(4,128)S(1)}, f32[5,4,1,384]{3,1,2,0:T(4,128)S(1)}, u32[]{:S(2)}, u32[]{:S(2)}) collective-permute-start(f32[5,4,1,384]{3,1,2,0:T(4,128)S(1)} %copy.428), channel_id=1, source_target_pairs={{0,16},{16,32},{32,48},{48,64},{64,80},{80,96},{96,112},{1,17},{17... | collective-permute-start | bytes 92168 | tf_op jit(solution)/shard_map/ppermute | solution.py:20
  230.1 6.0 %copy-start.5 = (f32[4,48,384]{2,1,0:T(8,128)S(1)}, f32[4,48,384]{2,1,0:T(8,128)}, u32[]{:S(2)}) copy-start(f32[4,48,384]{2,1,0:T(8,128)} %get-tuple-element.62) | copy-start | bytes 884740
  230.1 6.0 %copy-start.6 = (f32[4,48,384]{2,1,0:T(8,128)S(1)}, f32[4,48,384]{2,1,0:T(8,128)}, u32[]{:S(2)}) copy-start(f32[4,48,384]{2,1,0:T(8,128)} %get-tuple-element.63) | copy-start | bytes 884740
  230.1 6.0 %copy-start.7 = (f32[4,48,384]{2,1,0:T(8,128)S(1)}, f32[4,48,384]{2,1,0:T(8,128)}, u32[]{:S(2)}) copy-start(f32[4,48,384]{2,1,0:T(8,128)} %param.12) | copy-start | bytes 884740
  230.1 6.0 %copy-start.8 = (f32[48,384]{1,0:T(8,128)S(1)}, f32[48,384]{1,0:T(8,128)}, u32[]{:S(2)}) copy-start(f32[48,384]{1,0:T(8,128)} %multiply_add_fusion.4) | copy-start | bytes 221188
  230.1 5.6 %collective-permute-start.14 = (f32[5,4,1,384]{3,1,2,0:T(4,128)S(1)}, f32[5,4,1,384]{3,1,2,0:T(4,128)S(1)}, u32[]{:S(2)}, u32[]{:S(2)}) collective-permute-start(f32[5,4,1,384]{3,1,2,0:T(4,128)S(1)} %copy.430), channel_id=1, source_target_pairs={{16,0},{32,16},{48,32},{64,48},{80,64},{96,80},{112,96},{17,1},{33... | collective-permute-start | bytes 92168 | tf_op jit(solution)/shard_map/ppermute | solution.py:21
  238.4 16.6 %collective-permute-start.19 = (f32[5,4,48,1]{3,2,1,0:T(8,128)S(1)}, f32[5,4,48,1]{3,2,1,0:T(8,128)S(1)}, u32[]{:S(2)}, u32[]{:S(2)}) collective-permute-start(f32[5,4,48,1]{3,2,1,0:T(8,128)S(1)} %get-tuple-element.16), channel_id=1, source_target_pairs={{0,1},{1,2},{2,3},{3,4},{4,5},{5,6},{6,7},{7,8},{8,9},{9,10},{10,1... | collective-permute-start | bytes 11528 | tf_op jit(solution)/shard_map/ppermute | solution.py:22
  241.3 13.7 %collective-permute-start.20 = (f32[5,4,48,1]{3,2,1,0:T(8,128)S(1)}, f32[5,4,48,1]{3,2,1,0:T(8,128)S(1)}, u32[]{:S(2)}, u32[]{:S(2)}) collective-permute-start(f32[5,4,48,1]{3,2,1,0:T(8,128)S(1)} %get-tuple-element.17), channel_id=1, source_target_pairs={{1,0},{2,1},{3,2},{4,3},{5,4},{6,5},{7,6},{8,7},{9,8},{10,9},{11,1... | collective-permute-start | bytes 11528 | tf_op jit(solution)/shard_map/ppermute | solution.py:23
  244.4 7.7 %collective-permute-start.17 = (f32[5,4,1,384]{3,1,2,0:T(4,128)S(1)}, f32[5,4,1,384]{3,1,2,0:T(4,128)S(1)}, u32[]{:S(2)}, u32[]{:S(2)}) collective-permute-start(f32[5,4,1,384]{3,1,2,0:T(4,128)S(1)} %copy.433), channel_id=1, source_target_pairs={{0,16},{16,32},{32,48},{48,64},{64,80},{80,96},{96,112},{1,17},{17... | collective-permute-start | bytes 92168 | tf_op jit(solution)/shard_map/ppermute | solution.py:20
  249.5 5.5 %collective-permute-start.18 = (f32[5,4,1,384]{3,1,2,0:T(4,128)S(1)}, f32[5,4,1,384]{3,1,2,0:T(4,128)S(1)}, u32[]{:S(2)}, u32[]{:S(2)}) collective-permute-start(f32[5,4,1,384]{3,1,2,0:T(4,128)S(1)} %copy.435), channel_id=1, source_target_pairs={{16,0},{32,16},{48,32},{64,48},{80,64},{96,80},{112,96},{17,1},{33... | collective-permute-start | bytes 92168 | tf_op jit(solution)/shard_map/ppermute | solution.py:21
  256.8 1.1 copy-start.4
  341.5 28.9 %all-to-all-start = ((f32[5,4,128,128]{3,1,0,2:T(4,128)}), f32[5,4,128,128]{3,1,0,2:T(4,128)S(1)}, u32[]{:S(2)}, u32[]{:S(2)}) async-start(f32[5,4,128,128]{3,1,0,2:T(4,128)} %copy.438), calls=%async_computation | async-start | bytes 2621440 | tf_op jit(solution)/shard_map/all_to_all | solution.py:152
  370.6 46.9 %collective-permute-start.21 = (f32[5,4,48,128]{3,2,1,0:T(8,128)S(1)}, f32[5,4,48,128]{3,2,1,0:T(8,128)S(1)}, u32[]{:S(2)}, u32[]{:S(2)}) collective-permute-start(f32[5,4,48,128]{3,2,1,0:T(8,128)S(1)} %copy.439), channel_id=1, source_target_pairs={{1,9},{4,10},{7,11},{10,12},{13,13},{17,25},{20,26},{23,27},{26,28... | collective-permute-start | bytes 1474568 | tf_op jit(solution)/shard_map/ppermute | solution.py:163
  371.9 45.6 %collective-permute-start.22 = (f32[5,4,48,128]{3,2,1,0:T(8,128)S(1)}, f32[5,4,48,128]{3,2,1,0:T(8,128)S(1)}, u32[]{:S(2)}, u32[]{:S(2)}) collective-permute-start(f32[5,4,48,128]{3,2,1,0:T(8,128)S(1)} %copy.439), channel_id=1, source_target_pairs={{2,9},{5,10},{8,11},{11,12},{14,13},{18,25},{21,26},{24,27},{27,28... | collective-permute-start | bytes 1474568 | tf_op jit(solution)/shard_map/ppermute | solution.py:163
  373.9 43.8 %collective-permute-start.23 = (f32[5,4,48,128]{3,2,1,0:T(8,128)S(1)}, f32[5,4,48,128]{3,2,1,0:T(8,128)S(1)}, u32[]{:S(2)}, u32[]{:S(2)}) collective-permute-start(f32[5,4,48,128]{3,2,1,0:T(8,128)S(1)} %copy.439), channel_id=1, source_target_pairs={{0,8},{3,9},{6,10},{9,11},{12,12},{15,13},{16,24},{19,25},{22,26},... | collective-permute-start | bytes 1474568 | tf_op jit(solution)/shard_map/ppermute | solution.py:163
  380.3 37.3 %collective-permute-start.24 = (f32[5,4,48,128]{3,2,1,0:T(8,128)S(1)}, f32[5,4,48,128]{3,2,1,0:T(8,128)S(1)}, u32[]{:S(2)}, u32[]{:S(2)}) collective-permute-start(f32[5,4,48,128]{3,2,1,0:T(8,128)S(1)} %copy.439), channel_id=1, source_target_pairs={{1,8},{4,9},{7,10},{10,11},{13,12},{17,24},{20,25},{23,26},{26,27}... | collective-permute-start | bytes 1474568 | tf_op jit(solution)/shard_map/ppermute | solution.py:163
  381.7 47.6 %collective-permute-start.25 = (f32[5,4,48,128]{3,2,1,0:T(8,128)S(1)}, f32[5,4,48,128]{3,2,1,0:T(8,128)S(1)}, u32[]{:S(2)}, u32[]{:S(2)}) collective-permute-start(f32[5,4,48,128]{3,2,1,0:T(8,128)S(1)} %copy.439), channel_id=1, source_target_pairs={{2,8},{5,9},{8,10},{11,11},{14,12},{18,24},{21,25},{24,26},{27,27}... | collective-permute-start | bytes 1474568 | tf_op jit(solution)/shard_map/ppermute | solution.py:163
  417.6 11.7 %copy-start.3 = (f32[5,4,48,384]{3,2,1,0:T(8,128)S(1)}, f32[5,4,48,384]{3,2,1,0:T(8,128)}, u32[]{:S(2)}) copy-start(f32[5,4,48,384]{3,2,1,0:T(8,128)} %copy-done.2) | copy-start | bytes 4423684
Sparse Core Ops, SparseCore 0:
  118.2 88.0 all-reduce.5
